TPU v7x, 256 devices: a whole 4x4x8 slice. The times are simulated.
256 devices in a mesh: pb: 8 (over x, core), ka: 32 (over z, y).
Axes of the slice: x: 4, y: 4, z: 8, core: 2. Of those that a mesh axis runs over, the one named last changes fastest.
Arguments:
- queries: bfloat16 [32768, 512], P(('pb', 'ka')), may hold values from -9 to 9
- keys: bfloat16 [32768, 512], P(('ka', 'pb')), may hold values from -6 to 6
- values: bfloat16 [32768, 512], P(('ka', 'pb')), may hold values from -6 to 6
- block_pairs: int32 [6400, 2], replicated, may hold values from 0 to 255, as said below
- doc_lengths: int32 [16], replicated, may hold values from 1 to 8192, 32768 in all
Outputs:
- attended: bfloat16 [32768, 512], P(('pb', 'ka'))
Inputs may be any that keep to these rules, and one draw needn't show every extreme that they name: `block_pairs`: each row is (query block, key block) with the key block at most the query block; rows come grouped by query block, 25 rows each, and the first row of each group is the block with itself; a pair may appear more than once.
All inputs are finite; a program needn't handle non-finite values.
Results may differ from a plain program's by a relative error of at most 0.02.
Values may be sent and summed in bfloat16 or wider, within the bound.
No kernel may reach another device: no remote copies, remote signals or barrier semaphores. Data moves between devices by JAX's collectives and lax.ppermute only.
A program may use at most 64 MiB of HBM per device.

v0:
```python
import functools
import math

import jax
import jax.numpy as jnp
from jax import lax
from jax.experimental import pallas as pl
from jax.experimental.pallas import tpu as pltpu
from jax.sharding import Mesh
from jax.sharding import PartitionSpec as P

H = 4
DH = 128
BLK = 128
NX, NC, NZ, NY = 4, 2, 8, 4
PLANE = 32
NQ = NX * NY
PLANES = 3
NK = PLANES * NY * NC
STAT_ROWS = 16
ROWS = DH + STAT_ROWS
UNROLL = 8
COUNT_AT = NQ * NK // 2 + UNROLL
QUERY_AT = COUNT_AT + 1
KEY_AT = QUERY_AT + NQ
PLAN = KEY_AT + NK + 1
NOWHERE = 1 << 20
NEG = -1e30
SCALE = math.log2(math.e) / math.sqrt(DH)


def device(x, c, z, y):
    return ((x * NC + c) * NZ + z) * NY + y


PLACE = [
    [5, 3, 1, 0, 6, 2, 4, 7],
    [5, 4, 7, 3, 1, 0, 6, 2],
    [7, 5, 6, 1, 3, 2, 0, 4],
    [0, 6, 7, 4, 5, 1, 3, 2],
    [2, 7, 0, 1, 3, 6, 5, 4],
    [5, 3, 2, 7, 1, 0, 6, 4],
    [7, 6, 4, 5, 3, 2, 1, 0],
    [5, 1, 7, 6, 0, 3, 4, 2],
]
LIVES = [
    [
        sum(PLACE[(z + 1) % NZ].index(2 * x + c) << (3 * z) for z in range(NZ))
        for c in range(NC)
    ]
    for x in range(NX)
]


def transpose_pairs(back):
    pairs = []
    for x in range(NX):
        for c in range(NC):
            for z in range(NZ):
                for y in range(NY):
                    p = 2 * x + c
                    home = device(x, c, z, y)
                    work = device(PLACE[p][z] // 2, PLACE[p][z] % 2, (p - 1) % NZ, y)
                    pairs.append((work, home) if back else (home, work))
    return pairs


def ring(n, d):
    return [(i, (i + d) % n) for i in range(n)]


def pack_queries_kernel(q_ref, out_ref):
    for h in range(H):
        part = q_ref[:, h * DH : (h + 1) * DH].astype(jnp.float32).T.astype(jnp.bfloat16)
        for x in range(NX):
            out_ref[x * H + h] = part


def pack_keys_kernel(y_ref, k_hbm, v_hbm, *refs):
    out_refs, (k_ref, v_ref, sems) = refs[:NY], refs[NY:]
    copies = [
        pltpu.make_async_copy(v_hbm, v_ref, sems.at[0]),
        pltpu.make_async_copy(k_hbm, k_ref, sems.at[1]),
    ]
    for copy in copies:
        copy.start()
    for copy in copies:
        copy.wait()
    for d, out_ref in enumerate(out_refs):
        at = pl.ds(pl.multiple_of(lax.rem(y_ref[0] + d, H) * DH, DH), DH)
        out_ref[0] = k_ref[:, at]
        out_ref[1] = v_ref[:, at].astype(jnp.float32).T.astype(jnp.bfloat16)


def join_kernel(*refs):
    at = 0
    for ref in refs[:-1]:
        refs[-1][at : at + ref.shape[0]] = ref[...]
        at += ref.shape[0]


def join(parts):
    count = sum(p.shape[0] for p in parts)
    return pl.pallas_call(
        join_kernel,
        out_shape=jax.ShapeDtypeStruct((count,) + parts[0].shape[1:], parts[0].dtype),
        in_specs=[VMEM] * len(parts),
        out_specs=VMEM,
        compiler_params=SMALL,
        cost_estimate=LIGHT,
    )(*parts)


def lowest_bit(mask):
    return 31 - lax.clz(mask & -mask)


def plan_kernel(need_ref, qblk_ref, kblk_ref, plan_ref):
    def list_row(j, count):
        plan_ref[QUERY_AT + j] = qblk_ref[j]

        def entry(carry):
            mask, count = carry
            rest = mask & (mask - 1)
            second = jnp.where(rest == 0, NK, lowest_bit(rest))
            plan_ref[count] = j * 1024 + lowest_bit(mask) * 32 + second
            return rest & (rest - 1), count + 1

        return lax.while_loop(lambda c: c[0] != 0, entry, (need_ref[j], count))[1]

    count = lax.fori_loop(0, NQ, list_row, jnp.int32(0))
    for u in range(UNROLL):
        plan_ref[count + u] = NQ * 1024 + NK * 32 + NK
    plan_ref[COUNT_AT] = count
    for s in range(NK):
        plan_ref[KEY_AT + s] = kblk_ref[s]
    plan_ref[KEY_AT + NK] = NOWHERE


def attend_kernel(plan_ref, start_ref, q_ref, kv_ref, out_ref, acc, top, total):
    acc[...] = jnp.zeros_like(acc)
    top[...] = jnp.full_like(top, NEG)
    total[...] = jnp.zeros_like(total)
    key_row = lax.broadcasted_iota(jnp.int32, (BLK, BLK), 0)
    lane = lax.broadcasted_iota(jnp.int32, (1, BLK), 1)

    def step(first, width):
        done = []
        for u in range(width):
            entry = plan_ref[first + u]
            j = lax.shift_right_logical(entry, 10)
            jq = jnp.minimum(j, NQ - 1)
            slots = (lax.shift_right_logical(entry, 5) & 31, entry & 31)
            held = [jnp.minimum(s, NK - 1) for s in slots]
            scores = jnp.dot(
                jnp.concatenate([kv_ref[s, 0] for s in held], axis=0),
                q_ref[jq],
                preferred_element_type=jnp.float32,
            )
            masked = []
            for n, s in enumerate(slots):
                base = plan_ref[KEY_AT + s] * BLK
                low = start_ref[pl.ds(jq, 1), :] - base
                high = plan_ref[QUERY_AT + jq] * BLK + lane - base
                allowed = (key_row >= low) & (key_row <= high)
                part = scores[n * BLK : (n + 1) * BLK]
                masked.append(jnp.where(allowed, part * SCALE, NEG))
            scores = jnp.concatenate(masked, axis=0)
            peak = jnp.max(scores, axis=0, keepdims=True)
            weights = jnp.exp2(scores - peak)
            mass = jnp.sum(weights, axis=0, keepdims=True)
            part = jnp.dot(
                jnp.concatenate([kv_ref[s, 1] for s in held], axis=1),
                weights.astype(jnp.bfloat16),
                preferred_element_type=jnp.float32,
            )
            done.append((j, peak, mass, part))
        for j, peak, mass, part in done:
            at = pl.ds(j, 1)
            old = top[at, :]
            new = jnp.maximum(old, peak)
            keep = jnp.exp2(old - new)
            gain = jnp.exp2(peak - new)
            top[at, :] = new
            total[at, :] = total[at, :] * keep + mass * gain
            acc[j] = acc[j] * keep + part * gain

    def wide(i, carry):
        step(i * (2 * UNROLL), 2 * UNROLL)
        return carry

    turns = (plan_ref[COUNT_AT] + UNROLL - 1) // UNROLL
    lax.fori_loop(0, turns // 2, wide, 0)

    @pl.when(turns % 2 == 1)
    def _():
        step((turns - 1) * UNROLL, UNROLL)

    mass = total[:NQ, :]
    some = mass > 0.0
    safe = jnp.where(some, mass, 1.0)
    inverse = 1.0 / safe
    level = jnp.where(some, top[:NQ, :] + jnp.log2(safe), NEG)
    first = level.astype(jnp.bfloat16).astype(jnp.float32)
    second = (level - first).astype(jnp.bfloat16).astype(jnp.float32)
    third = level - first - second
    row = lax.broadcasted_iota(jnp.int32, (STAT_ROWS, BLK), 0)
    for j in range(NQ):
        one = slice(j, j + 1)
        out_ref[j, :DH, :] = (acc[j] * inverse[one]).astype(jnp.bfloat16)
        stat = jnp.where(
            row == 0, first[one], jnp.where(row == 1, second[one], third[one])
        )
        out_ref[j, DH:, :] = jnp.where(row < 3, stat, 0.0).astype(jnp.bfloat16)


def combine_kernel(parts_ref, out_ref):
    for h in range(H):
        levels = []
        for r in range(NX):
            stat = parts_ref[r * H + h, DH:, :].astype(jnp.float32)
            levels.append(stat[0:1] + stat[1:2] + stat[2:3])
        peak = functools.reduce(jnp.maximum, levels)
        shares = [jnp.exp2(level - peak) for level in levels]
        inverse = 1.0 / functools.reduce(jnp.add, shares)
        value = functools.reduce(
            jnp.add,
            [
                parts_ref[r * H + h, :DH, :].astype(jnp.float32) * (shares[r] * inverse)
                for r in range(NX)
            ],
        )
        out_ref[:, h * DH : (h + 1) * DH] = value.T.astype(jnp.bfloat16)


VMEM = pl.BlockSpec(memory_space=pltpu.VMEM)
SMEM = pl.BlockSpec(memory_space=pltpu.SMEM)
LIGHT = pl.CostEstimate(flops=1024, bytes_accessed=1024, transcendentals=0)
HBM = pl.BlockSpec(memory_space=pltpu.HBM)
SMALL = pltpu.CompilerParams(vmem_limit_bytes=8 << 20)


def on_device(queries, keys, values, block_pairs, doc_lengths):
    x, c, z, y = (lax.axis_index(name) for name in ("x", "c", "z", "y"))
    bf16 = jnp.bfloat16

    piece = jax.ShapeDtypeStruct((2, BLK, DH), bf16)
    split = pl.pallas_call(
        pack_keys_kernel,
        out_shape=[piece] * NY,
        in_specs=[SMEM, HBM, HBM],
        out_specs=[VMEM] * NY,
        scratch_shapes=[pltpu.VMEM((BLK, H * DH), bf16)] * 2 + [pltpu.SemaphoreType.DMA((2,))],
        compiler_params=SMALL,
        cost_estimate=LIGHT,
    )(
        y.reshape(1),
        pltpu.with_memory_space_constraint(keys, pltpu.HBM),
        pltpu.with_memory_space_constraint(values, pltpu.HBM),
    )
    moved = lax.ppermute(queries, ("x", "c", "z", "y"), transpose_pairs(False))
    pieces = [split[0]] + [lax.ppermute(split[d], "y", ring(NY, d)) for d in range(1, NY)]
    here = join([p[None] for p in pieces])
    moved, here = lax.optimization_barrier((moved, here))

    spread = pl.pallas_call(
        pack_queries_kernel,
        out_shape=jax.ShapeDtypeStruct((NQ, DH, BLK), bf16),
        in_specs=[VMEM],
        out_specs=VMEM,
        compiler_params=SMALL,
        cost_estimate=LIGHT,
    )(moved)
    mine = lax.all_to_all(spread, ("x", "y"), 0, 0, tiled=True)
    near = [here, lax.ppermute(here, "z", ring(NZ, 1)), lax.ppermute(here, "z", ring(NZ, -1))]
    near[0], near[1], block_pairs, doc_lengths, x, c, z, y = lax.optimization_barrier(
        (near[0], near[1], block_pairs, doc_lengths, x, c, z, y)
    )
    other = [lax.ppermute(b, "c", ring(NC, 1)) for b in near]

    slot = jnp.arange(NQ, dtype=jnp.int32)
    digits = [
        lax.shift_right_logical(jnp.where(c == 0, LIVES[n][0], LIVES[n][1]), 3 * z) & 7
        for n in range(NX)
    ]
    lives = functools.reduce(
        lambda rest, n: jnp.where(slot // NY == n, digits[n], rest), range(NX), slot
    )
    query_block = PLANE * lax.rem(z + 1, NZ) + NY * lives + slot % NY
    slot = jnp.arange(NK, dtype=jnp.int32)
    group = (slot // NY) % PLANES
    plane = lax.rem(z + jnp.where(group == 0, 0, jnp.where(group == 1, NZ - 1, 1)), NZ)
    row = lax.rem(y + NY - slot % NY, NY)
    core = jnp.where(slot < PLANES * NY, c, 1 - c)
    key_block = PLANE * plane + 8 * row + 2 * x + core
    ends = jnp.sum(
        jnp.where(
            jnp.arange(16)[:, None] <= jnp.arange(16)[None, :], doc_lengths[:, None], 0
        ),
        axis=0,
    )
    token = query_block[:, None] * BLK + jnp.arange(BLK, dtype=jnp.int32)[None, :]
    start = jnp.max(jnp.where(ends[:, None, None] <= token[None], ends[:, None, None], 0), axis=0)
    first = jnp.max(
        jnp.where(ends[:, None] <= query_block[None] * BLK, ends[:, None], 0), axis=0
    )
    hit_query = (block_pairs[:, 0][None, :] == query_block[:, None]).astype(bf16)
    hit_key = (block_pairs[:, 1][None, :] == key_block[:, None]).astype(bf16)
    listed = lax.dot_general(
        hit_query, hit_key, (((1,), (1,)), ((), ())), preferred_element_type=jnp.float32
    )
    need = (
        (listed > 0.5)
        & (key_block[None, :] * BLK + (BLK - 1) >= first[:, None])
        & (key_block[None, :] <= query_block[:, None])
    )
    bits = jnp.left_shift(jnp.int32(1), jnp.arange(NK, dtype=jnp.int32))
    need = jnp.sum(jnp.where(need, bits[None, :], 0), axis=1)

    plan = pl.pallas_call(
        plan_kernel,
        out_shape=jax.ShapeDtypeStruct((PLAN,), jnp.int32),
        in_specs=[SMEM] * 3,
        out_specs=SMEM,
        compiler_params=SMALL,
        cost_estimate=LIGHT,
    )(need, query_block, key_block)
    parts = pl.pallas_call(
        attend_kernel,
        out_shape=jax.ShapeDtypeStruct((NQ, ROWS, BLK), bf16),
        in_specs=[SMEM, VMEM, VMEM, VMEM],
        out_specs=VMEM,
        scratch_shapes=[
            pltpu.VMEM((NQ + 1, DH, BLK), jnp.float32),
            pltpu.VMEM((NQ + 8, BLK), jnp.float32),
            pltpu.VMEM((NQ + 8, BLK), jnp.float32),
        ],
        compiler_params=pltpu.CompilerParams(vmem_limit_bytes=24 << 20),
    )(plan, start, mine, join([*near, *other]))

    gathered = lax.all_to_all(parts, ("x", "y"), 0, 0, tiled=True)
    result = pl.pallas_call(
        combine_kernel,
        out_shape=jax.ShapeDtypeStruct((BLK, H * DH), bf16),
        in_specs=[VMEM],
        out_specs=VMEM,
        compiler_params=SMALL,
        cost_estimate=LIGHT,
    )(gathered)
    return lax.ppermute(result, ("x", "c", "z", "y"), transpose_pairs(True))


def solution(mesh):
    fine = Mesh(mesh.devices.reshape(NX, NC, NZ, NY), ("x", "c", "z", "y"))
    return jax.shard_map(
        on_device,
        mesh=fine,
        in_specs=(
            P(("x", "c", "z", "y"), None),
            P(("z", "y", "x", "c"), None),
            P(("z", "y", "x", "c"), None),
            P(),
            P(),
        ),
        out_specs=P(("x", "c", "z", "y"), None),
        check_vma=False,
    )
```

profile of v0, /device:TPU:8, one launch (start us, length us, event | category | flops | bytes accessed | tf_op | source)
XLA Modules:
  0.0 62.8 jit_solution(5647451346620262315)
XLA Ops:
  0.0 0.0 copy-start
  0.0 0.0 copy-start.1
  0.0 7.8 %collective-permute-start = (bf16[128,512]{1,0:T(8,128)(2,1)}, bf16[128,512]{1,0:T(8,128)(2,1)S(1)}, u32[]{:S(2)}, u32[]{:S(2)}) collective-permute-start(bf16[128,512]{1,0:T(8,128)(2,1)} %param.5), channel_id=1, source_target_pairs={{0,188},{1,189},{2,190},{3,191},{4,124},{5,125},{6,126},{7,127},{8... | collective-permute-start | bytes 393224 | tf_op jit(solution)/shard_map/ppermute | solution.py:261
  7.8 1.1 %shard_map.55 = (bf16[2,128,128]{2,1,0:T(8,128)(2,1)S(1)}, bf16[2,128,128]{2,1,0:T(8,128)(2,1)S(1)}, bf16[2,128,128]{2,1,0:T(8,128)(2,1)S(1)}, bf16[2,128,128]{2,1,0:T(8,128)(2,1)S(1)}) custom-call(s32[1]{0:T(128)} %bitcast.y_ref, bf16[128,512]{1,0:T(8,128)(2,1)} %k_hbm.1, bf16[128,512]{1,0:T(8,128)(2,1)} %v_hbm.1), custom_call_target="tpu_custom_call" | custom-call | flops 1024 | bytes 1024 | tf_op jit(solution)/shard_map/pallas_call | solution.py:248
  8.9 1.7 %collective-permute-start.1 = (bf16[2,128,128]{2,1,0:T(8,128)(2,1)S(1)}, bf16[2,128,128]{2,1,0:T(8,128)(2,1)S(1)}, u32[]{:S(2)}, u32[]{:S(2)}) collective-permute-start(bf16[2,128,128]{2,1,0:T(8,128)(2,1)S(1)} %get-tuple-element.20), channel_id=1, source_target_pairs={{0,1},{1,2},{2,3},{3,0},{4,5},{5,6},{6,7},{7,4},{8,9},{9,10},{10,1... | collective-permute-start | bytes 196616 | tf_op jit(solution)/shard_map/ppermute | solution.py:262
  10.5 0.9 %collective-permute-start.2 = (bf16[2,128,128]{2,1,0:T(8,128)(2,1)S(1)}, bf16[2,128,128]{2,1,0:T(8,128)(2,1)S(1)}, u32[]{:S(2)}, u32[]{:S(2)}) collective-permute-start(bf16[2,128,128]{2,1,0:T(8,128)(2,1)S(1)} %get-tuple-element.21), channel_id=1, source_target_pairs={{0,2},{1,3},{2,0},{3,1},{4,6},{5,7},{6,4},{7,5},{8,10},{9,11},{10,... | collective-permute-start | bytes 196616 | tf_op jit(solution)/shard_map/ppermute | solution.py:262
  11.5 2.4 %collective-permute-start.3 = (bf16[2,128,128]{2,1,0:T(8,128)(2,1)S(1)}, bf16[2,128,128]{2,1,0:T(8,128)(2,1)S(1)}, u32[]{:S(2)}, u32[]{:S(2)}) collective-permute-start(bf16[2,128,128]{2,1,0:T(8,128)(2,1)S(1)} %get-tuple-element.22), channel_id=1, source_target_pairs={{0,3},{1,0},{2,1},{3,2},{4,7},{5,4},{6,5},{7,6},{8,11},{9,8},{10,9... | collective-permute-start | bytes 196616 | tf_op jit(solution)/shard_map/ppermute | solution.py:262
  13.9 0.0 collective-permute-done.1
  13.9 2.5 %collective-permute-done.2 = bf16[2,128,128]{2,1,0:T(8,128)(2,1)S(1)} collective-permute-done((bf16[2,128,128]{2,1,0:T(8,128)(2,1)S(1)}, bf16[2,128,128]{2,1,0:T(8,128)(2,1)S(1)}, u32[]{:S(2)}, u32[]{:S(2)}) %collective-permute-start.2) | collective-permute-done | bytes 65568 | tf_op jit(solution)/shard_map/ppermute | solution.py:262
  16.4 0.0 collective-permute-done.3
  16.5 0.0 collective-permute-done.q_ref
  16.5 0.1 collective-permute-start.4
  16.6 3.2 %collective-permute-start.5 = (bf16[4,2,128,128]{3,2,1,0:T(8,128)(2,1)S(1)}, bf16[4,2,128,128]{3,2,1,0:T(8,128)(2,1)S(1)}, u32[]{:S(2)}, u32[]{:S(2)}) collective-permute-start(bf16[4,2,128,128]{3,2,1,0:T(8,128)(2,1)S(1)} %shard_map.56.refs_0_), channel_id=1, source_target_pairs={{0,28},{4,0},{8,4},{12,8},{16,12},{20,16},{24,20},{28,24},{1,29},{... | collective-permute-start | bytes 786440 | tf_op jit(solution)/shard_map/ppermute | solution.py:275
  19.8 0.9 %shard_map.58 = bf16[16,128,128]{2,1,0:T(8,128)(2,1)} custom-call(bf16[128,512]{1,0:T(8,128)(2,1)S(1)} %collective-permute-done.q_ref), custom_call_target="tpu_custom_call" | custom-call | flops 1024 | bytes 1024 | tf_op jit(solution)/shard_map/pallas_call | solution.py:266
  20.7 6.2 %all-to-all-start = ((bf16[16,128,128]{2,1,0:T(8,128)(2,1)}), bf16[16,128,128]{2,1,0:T(8,128)(2,1)S(1)}, u32[]{:S(2)}, u32[]{:S(2)}) async-start(bf16[16,128,128]{2,1,0:T(8,128)(2,1)} %shard_map.58), calls=%async_computation | async-start | bytes 1048576 | tf_op jit(solution)/shard_map/all_to_all | solution.py:274
  26.9 0.0 collective-permute-done.4.refs_1_
  26.9 0.1 collective-permute-start.6
  27.0 0.0 copy-done.1
  27.0 0.1 select_reduce_fusion.2
  27.1 0.0 copy-done
  27.1 0.1 slice_reduce_fusion.1
  27.3 0.1 select_reduce_fusion.1
  27.4 0.4 fusion.3.need_ref
  27.8 0.6 collective-permute-start.7
  28.4 1.5 %shard_map.57.plan_ref = s32[242]{0:T(256)S(1)} custom-call(s32[16]{0:T(128)S(1)} %fusion.3.need_ref, s32[16]{0:T(128)S(1)} %get-tuple-element.36.qblk_ref, s32[24]{0:T(128)S(1)} %get-tuple-element.38.kblk_ref), custom_call_target="tpu_custom_call" | custom-call | flops 1024 | bytes 1024 | tf_op jit(solution)/shard_map/pallas_call | solution.py:320
  29.8 0.0 collective-permute-done.5.refs_2_
  29.9 0.2 collective-permute-start.8
  30.1 0.1 iota_add_fusion
  30.1 0.1 select_reduce_fusion.start_ref
  30.2 0.0 collective-permute-done.6.refs_3_
  30.2 0.0 collective-permute-done.7.refs_4_
  30.3 1.2 %collective-permute-done.8.refs_5_ = bf16[4,2,128,128]{3,2,1,0:T(8,128)(2,1)S(1)} collective-permute-done((bf16[4,2,128,128]{3,2,1,0:T(8,128)(2,1)S(1)}, bf16[4,2,128,128]{3,2,1,0:T(8,128)(2,1)S(1)}, u32[]{:S(2)}, u32[]{:S(2)}) %collective-permute-start.8) | collective-permute-done | bytes 262176 | tf_op jit(solution)/shard_map/ppermute | solution.py:279
  31.5 0.1 shard_map.59.kv_ref
  31.6 5.3 %all-to-all-done.q_ref = bf16[16,128,128]{2,1,0:T(8,128)(2,1)S(1)} async-done(((bf16[16,128,128]{2,1,0:T(8,128)(2,1)}), bf16[16,128,128]{2,1,0:T(8,128)(2,1)S(1)}, u32[]{:S(2)}, u32[]{:S(2)}) %all-to-all-start) | async-done | bytes 524320 | tf_op jit(solution)/shard_map/all_to_all | solution.py:274
  36.9 2.1 %shard_map.60 = bf16[16,144,128]{2,1,0:T(8,128)(2,1)S(1)} custom-call(s32[242]{0:T(256)S(1)} %shard_map.57.plan_ref, s32[16,128]{1,0:T(8,128)S(1)} %select_reduce_fusion.start_ref, bf16[16,128,128]{2,1,0:T(8,128)(2,1)S(1)} %all-to-all-done.q_ref, bf16[24,2,128,128]{3,2,1,0:T(8,128)(2,1)S(1)} %shard_map.59.kv_ref), custom_call_target="tpu_custom_call" | custom-call | tf_op jit(solution)/shard_map/pallas_call | solution.py:328
  39.0 14.4 %all_to_all.10.parts_ref = bf16[16,144,128]{2,1,0:T(8,128)(2,1)S(1)} all-to-all(bf16[16,144,128]{2,1,0:T(8,128)(2,1)S(1)} %shard_map.60), channel_id=1, replica_groups=mesh['x'=4,'c'=2,'z'=8,'y'=4] {'x','y'}, dimensions={0} | all-to-all | bytes 1179648 | tf_op jit(solution)/shard_map/all_to_all | solution.py:341
  53.3 0.2 shard_map.61
  53.5 0.1 collective-permute-start.9
  53.6 8.5 %collective-permute-done.9 = bf16[128,512]{1,0:T(8,128)(2,1)S(1)} collective-permute-done((bf16[128,512]{1,0:T(8,128)(2,1)S(1)}, bf16[128,512]{1,0:T(8,128)(2,1)S(1)}, u32[]{:S(2)}, u32[]{:S(2)}) %collective-permute-start.9) | collective-permute-done | bytes 131104 | tf_op jit(solution)/shard_map/ppermute | solution.py:350
  62.1 0.7 %copy.7 = bf16[128,512]{1,0:T(8,128)(2,1)} copy(bf16[128,512]{1,0:T(8,128)(2,1)S(1)} %collective-permute-done.9) | data formatting | bytes 262144
  (4 shorter events, 0.1 us)
Async XLA Ops:
  0.0 27.1 %copy-start = (s32[6400,2]{0,1:T(2,128)S(1)}, s32[6400,2]{0,1:T(2,128)}, u32[]{:S(2)}) copy-start(s32[6400,2]{0,1:T(2,128)} %param.8) | copy-start | bytes 153604
  0.0 27.0 %copy-start.1 = (s32[16]{0:T(128)S(1)}, s32[16]{0:T(128)}, u32[]{:S(2)}) copy-start(s32[16]{0:T(128)} %param.9) | copy-start | bytes 196
  0.0 16.5 %collective-permute-start = (bf16[128,512]{1,0:T(8,128)(2,1)}, bf16[128,512]{1,0:T(8,128)(2,1)S(1)}, u32[]{:S(2)}, u32[]{:S(2)}) collective-permute-start(bf16[128,512]{1,0:T(8,128)(2,1)} %param.5), channel_id=1, source_target_pairs={{0,188},{1,189},{2,190},{3,191},{4,124},{5,125},{6,126},{7,127},{8... | collective-permute-start | bytes 393224 | tf_op jit(solution)/shard_map/ppermute | solution.py:261
  8.9 5.0 %collective-permute-start.1 = (bf16[2,128,128]{2,1,0:T(8,128)(2,1)S(1)}, bf16[2,128,128]{2,1,0:T(8,128)(2,1)S(1)}, u32[]{:S(2)}, u32[]{:S(2)}) collective-permute-start(bf16[2,128,128]{2,1,0:T(8,128)(2,1)S(1)} %get-tuple-element.20), channel_id=1, source_target_pairs={{0,1},{1,2},{2,3},{3,0},{4,5},{5,6},{6,7},{7,4},{8,9},{9,10},{10,1... | collective-permute-start | bytes 196616 | tf_op jit(solution)/shard_map/ppermute | solution.py:262
  10.5 5.9 %collective-permute-start.2 = (bf16[2,128,128]{2,1,0:T(8,128)(2,1)S(1)}, bf16[2,128,128]{2,1,0:T(8,128)(2,1)S(1)}, u32[]{:S(2)}, u32[]{:S(2)}) collective-permute-start(bf16[2,128,128]{2,1,0:T(8,128)(2,1)S(1)} %get-tuple-element.21), channel_id=1, source_target_pairs={{0,2},{1,3},{2,0},{3,1},{4,6},{5,7},{6,4},{7,5},{8,10},{9,11},{10,... | collective-permute-start | bytes 196616 | tf_op jit(solution)/shard_map/ppermute | solution.py:262
  11.5 5.0 %collective-permute-start.3 = (bf16[2,128,128]{2,1,0:T(8,128)(2,1)S(1)}, bf16[2,128,128]{2,1,0:T(8,128)(2,1)S(1)}, u32[]{:S(2)}, u32[]{:S(2)}) collective-permute-start(bf16[2,128,128]{2,1,0:T(8,128)(2,1)S(1)} %get-tuple-element.22), channel_id=1, source_target_pairs={{0,3},{1,0},{2,1},{3,2},{4,7},{5,4},{6,5},{7,6},{8,11},{9,8},{10,9... | collective-permute-start | bytes 196616 | tf_op jit(solution)/shard_map/ppermute | solution.py:262
  16.5 10.4 %collective-permute-start.4 = (bf16[4,2,128,128]{3,2,1,0:T(8,128)(2,1)S(1)}, bf16[4,2,128,128]{3,2,1,0:T(8,128)(2,1)S(1)}, u32[]{:S(2)}, u32[]{:S(2)}) collective-permute-start(bf16[4,2,128,128]{3,2,1,0:T(8,128)(2,1)S(1)} %shard_map.56.refs_0_), channel_id=1, source_target_pairs={{0,4},{4,8},{8,12},{12,16},{16,20},{20,24},{24,28},{28,0},{1,5},{5... | collective-permute-start | bytes 786440 | tf_op jit(solution)/shard_map/ppermute | solution.py:275
  16.6 13.3 %collective-permute-start.5 = (bf16[4,2,128,128]{3,2,1,0:T(8,128)(2,1)S(1)}, bf16[4,2,128,128]{3,2,1,0:T(8,128)(2,1)S(1)}, u32[]{:S(2)}, u32[]{:S(2)}) collective-permute-start(bf16[4,2,128,128]{3,2,1,0:T(8,128)(2,1)S(1)} %shard_map.56.refs_0_), channel_id=1, source_target_pairs={{0,28},{4,0},{8,4},{12,8},{16,12},{20,16},{24,20},{28,24},{1,29},{... | collective-permute-start | bytes 786440 | tf_op jit(solution)/shard_map/ppermute | solution.py:275
  20.7 16.2 %all-to-all-start = ((bf16[16,128,128]{2,1,0:T(8,128)(2,1)}), bf16[16,128,128]{2,1,0:T(8,128)(2,1)S(1)}, u32[]{:S(2)}, u32[]{:S(2)}) async-start(bf16[16,128,128]{2,1,0:T(8,128)(2,1)} %shard_map.58), calls=%async_computation | async-start | bytes 1048576 | tf_op jit(solution)/shard_map/all_to_all | solution.py:274
  26.9 3.3 %collective-permute-start.6 = (bf16[4,2,128,128]{3,2,1,0:T(8,128)(2,1)S(1)}, bf16[4,2,128,128]{3,2,1,0:T(8,128)(2,1)S(1)}, u32[]{:S(2)}, u32[]{:S(2)}) collective-permute-start(bf16[4,2,128,128]{3,2,1,0:T(8,128)(2,1)S(1)} %shard_map.56.refs_0_), channel_id=1, source_target_pairs={{0,32},{32,0},{1,33},{33,1},{2,34},{34,2},{3,35},{35,3},{4,36},{36... | collective-permute-start | bytes 786440 | tf_op jit(solution)/shard_map/ppermute | solution.py:279
  27.8 2.4 %collective-permute-start.7 = (bf16[4,2,128,128]{3,2,1,0:T(8,128)(2,1)S(1)}, bf16[4,2,128,128]{3,2,1,0:T(8,128)(2,1)S(1)}, u32[]{:S(2)}, u32[]{:S(2)}) collective-permute-start(bf16[4,2,128,128]{3,2,1,0:T(8,128)(2,1)S(1)} %collective-permute-done.4.refs_1_), channel_id=1, source_target_pairs={{0,32},{32,0},{1,33},{33,1},{2,34},{34,2},{3,35},{35,3},{4,36},{36... | collective-permute-start | bytes 786440 | tf_op jit(solution)/shard_map/ppermute | solution.py:279
  29.9 1.6 %collective-permute-start.8 = (bf16[4,2,128,128]{3,2,1,0:T(8,128)(2,1)S(1)}, bf16[4,2,128,128]{3,2,1,0:T(8,128)(2,1)S(1)}, u32[]{:S(2)}, u32[]{:S(2)}) collective-permute-start(bf16[4,2,128,128]{3,2,1,0:T(8,128)(2,1)S(1)} %collective-permute-done.5.refs_2_), channel_id=1, source_target_pairs={{0,32},{32,0},{1,33},{33,1},{2,34},{34,2},{3,35},{35,3},{4,36},{36... | collective-permute-start | bytes 786440 | tf_op jit(solution)/shard_map/ppermute | solution.py:279
  53.5 8.6 %collective-permute-start.9 = (bf16[128,512]{1,0:T(8,128)(2,1)S(1)}, bf16[128,512]{1,0:T(8,128)(2,1)S(1)}, u32[]{:S(2)}, u32[]{:S(2)}) collective-permute-start(bf16[128,512]{1,0:T(8,128)(2,1)S(1)} %shard_map.61), channel_id=1, source_target_pairs={{188,0},{189,1},{190,2},{191,3},{124,4},{125,5},{126,6},{127,7},{6... | collective-permute-start | bytes 393224 | tf_op jit(solution)/shard_map/ppermute | solution.py:350
where the time goes:
time: 62.9 us; the launch traced here: 62.8 us
  starting transfers between devices  23.2 us (37%)
  waiting for transfers between devices  17.6 us (28%)
  blocking collectives  14.4 us (23%)
  Pallas kernels  5.88 us (9%)
  local copies, waits for them, and re-layouts  0.78 us (1%)
    all_to_all x1, blocking collectives, on_device(): gathered = lax.all_to_all(parts, ('x', 'y'), 0, 0, tiled=True)  14.4 us
    ppermute x1, waiting for transfers between devices, on_device(): return lax.ppermute(result, ('x', 'c', 'z', 'y'), transpose_pairs(True))  8.49 us
    ppermute x1, starting transfers between devices, on_device(): moved = lax.ppermute(queries, ('x', 'c', 'z', 'y'), transpose_pairs(False))  7.76 us
    all_to_all x1, starting transfers between devices, on_device(): mine = lax.all_to_all(spread, ('x', 'y'), 0, 0, tiled=True)  6.18 us
    all_to_all x1, waiting for transfers between devices, on_device(): mine = lax.all_to_all(spread, ('x', 'y'), 0, 0, tiled=True)  5.3 us
    ppermute x3, starting transfers between devices, on_device(): lax.ppermute(split[d], 'y', ring(NY, d))  5 us
    ppermute x1, starting transfers between devices, on_device(): lax.ppermute(here, 'z', ring(NZ, -1))  3.21 us
    ppermute x3, waiting for transfers between devices, on_device(): lax.ppermute(split[d], 'y', ring(NY, d))  2.56 us
  transfers between devices with their start and end apart: 11, of which 4 were waited for; matrix products, arithmetic and copies ran while one was open for 1% of the time, Pallas kernels for 6%

commit v1 on v0

--- a/solution.py
+++ b/solution.py
@@ -265,7 +265,7 @@
 
     spread = pl.pallas_call(
         pack_queries_kernel,
-        out_shape=jax.ShapeDtypeStruct((NQ, DH, BLK), bf16),
+        out_shape=pltpu.VMEM((NQ, DH, BLK), bf16),
         in_specs=[VMEM],
         out_specs=VMEM,
         compiler_params=SMALL,
@@ -314,7 +314,7 @@
         & (key_block[None, :] * BLK + (BLK - 1) >= first[:, None])
         & (key_block[None, :] <= query_block[:, None])
     )
-    bits = jnp.left_shift(jnp.int32(1), jnp.arange(NK, dtype=jnp.int32))
+    bits = jnp.left_shift(jnp.int32(1), slot)
     need = jnp.sum(jnp.where(need, bits[None, :], 0), axis=1)
 
     plan = pl.pallas_call(

time: 62.9 us -> 62.9 us (level)
  Pallas kernels: 5.88 us -> 6.71 us
    pallas_call x1, Pallas kernels: 2.07 us -> 2.84 us  [on_device(): pl.pallas_call(attend_kernel, out_shape=jax.ShapeDtypeStruct((NQ, ROWS, B...]
where the time goes in v1:
time: 62.9 us; the launch traced here: 62.5 us
  starting transfers between devices  23.1 us (37%)
  waiting for transfers between devices  17.2 us (27%)
  blocking collectives  13.8 us (22%)
  Pallas kernels  6.71 us (11%)
  local copies, waits for them, and re-layouts  0.78 us (1%)
    all_to_all x1, blocking collectives, on_device(): gathered = lax.all_to_all(parts, ('x', 'y'), 0, 0, tiled=True)  13.8 us
    ppermute x1, waiting for transfers between devices, on_device(): return lax.ppermute(result, ('x', 'c', 'z', 'y'), transpose_pairs(True))  8.06 us
    ppermute x1, starting transfers between devices, on_device(): moved = lax.ppermute(queries, ('x', 'c', 'z', 'y'), transpose_pairs(False))  7.76 us
    all_to_all x1, starting transfers between devices, on_device(): mine = lax.all_to_all(spread, ('x', 'y'), 0, 0, tiled=True)  6.18 us
    all_to_all x1, waiting for transfers between devices, on_device(): mine = lax.all_to_all(spread, ('x', 'y'), 0, 0, tiled=True)  5.23 us
    ppermute x3, starting transfers between devices, on_device(): lax.ppermute(split[d], 'y', ring(NY, d))  5 us
    ppermute x1, starting transfers between devices, on_device(): lax.ppermute(here, 'z', ring(NZ, -1))  3.21 us
    pallas_call x1, Pallas kernels, on_device(): pl.pallas_call(attend_kernel, out_shape=jax.ShapeDtypeStruct((NQ, ROWS, B...  2.84 us
  transfers between devices with their start and end apart: 11, of which 4 were waited for; matrix products, arithmetic and copies ran while one was open for 1% of the time, Pallas kernels for 6%

profile of v1, /device:TPU:8, one launch (start us, length us, event | category | flops | bytes accessed | tf_op | source)
XLA Modules:
  0.0 62.5 jit_solution(5647451346620262315)
XLA Ops:
  0.0 0.0 copy-start
  0.0 0.0 copy-start.1
  0.0 7.8 %collective-permute-start = (bf16[128,512]{1,0:T(8,128)(2,1)}, bf16[128,512]{1,0:T(8,128)(2,1)S(1)}, u32[]{:S(2)}, u32[]{:S(2)}) collective-permute-start(bf16[128,512]{1,0:T(8,128)(2,1)} %param.5), channel_id=1, source_target_pairs={{0,188},{1,189},{2,190},{3,191},{4,124},{5,125},{6,126},{7,127},{8... | collective-permute-start | bytes 393224 | tf_op jit(solution)/shard_map/ppermute | solution.py:261
  7.8 1.1 %shard_map.55 = (bf16[2,128,128]{2,1,0:T(8,128)(2,1)S(1)}, bf16[2,128,128]{2,1,0:T(8,128)(2,1)S(1)}, bf16[2,128,128]{2,1,0:T(8,128)(2,1)S(1)}, bf16[2,128,128]{2,1,0:T(8,128)(2,1)S(1)}) custom-call(s32[1]{0:T(128)} %bitcast.y_ref, bf16[128,512]{1,0:T(8,128)(2,1)} %k_hbm.1, bf16[128,512]{1,0:T(8,128)(2,1)} %v_hbm.1), custom_call_target="tpu_custom_call" | custom-call | flops 1024 | bytes 1024 | tf_op jit(solution)/shard_map/pallas_call | solution.py:248
  8.9 1.7 %collective-permute-start.1 = (bf16[2,128,128]{2,1,0:T(8,128)(2,1)S(1)}, bf16[2,128,128]{2,1,0:T(8,128)(2,1)S(1)}, u32[]{:S(2)}, u32[]{:S(2)}) collective-permute-start(bf16[2,128,128]{2,1,0:T(8,128)(2,1)S(1)} %get-tuple-element.20), channel_id=1, source_target_pairs={{0,1},{1,2},{2,3},{3,0},{4,5},{5,6},{6,7},{7,4},{8,9},{9,10},{10,1... | collective-permute-start | bytes 196616 | tf_op jit(solution)/shard_map/ppermute | solution.py:262
  10.5 0.9 %collective-permute-start.2 = (bf16[2,128,128]{2,1,0:T(8,128)(2,1)S(1)}, bf16[2,128,128]{2,1,0:T(8,128)(2,1)S(1)}, u32[]{:S(2)}, u32[]{:S(2)}) collective-permute-start(bf16[2,128,128]{2,1,0:T(8,128)(2,1)S(1)} %get-tuple-element.21), channel_id=1, source_target_pairs={{0,2},{1,3},{2,0},{3,1},{4,6},{5,7},{6,4},{7,5},{8,10},{9,11},{10,... | collective-permute-start | bytes 196616 | tf_op jit(solution)/shard_map/ppermute | solution.py:262
  11.5 2.4 %collective-permute-start.3 = (bf16[2,128,128]{2,1,0:T(8,128)(2,1)S(1)}, bf16[2,128,128]{2,1,0:T(8,128)(2,1)S(1)}, u32[]{:S(2)}, u32[]{:S(2)}) collective-permute-start(bf16[2,128,128]{2,1,0:T(8,128)(2,1)S(1)} %get-tuple-element.22), channel_id=1, source_target_pairs={{0,3},{1,0},{2,1},{3,2},{4,7},{5,4},{6,5},{7,6},{8,11},{9,8},{10,9... | collective-permute-start | bytes 196616 | tf_op jit(solution)/shard_map/ppermute | solution.py:262
  13.9 0.0 collective-permute-done.1
  13.9 2.5 %collective-permute-done.2 = bf16[2,128,128]{2,1,0:T(8,128)(2,1)S(1)} collective-permute-done((bf16[2,128,128]{2,1,0:T(8,128)(2,1)S(1)}, bf16[2,128,128]{2,1,0:T(8,128)(2,1)S(1)}, u32[]{:S(2)}, u32[]{:S(2)}) %collective-permute-start.2) | collective-permute-done | bytes 65568 | tf_op jit(solution)/shard_map/ppermute | solution.py:262
  16.4 0.0 collective-permute-done.3
  16.5 0.0 collective-permute-done.q_ref
  16.5 0.1 collective-permute-start.4
  16.6 3.2 %collective-permute-start.5 = (bf16[4,2,128,128]{3,2,1,0:T(8,128)(2,1)S(1)}, bf16[4,2,128,128]{3,2,1,0:T(8,128)(2,1)S(1)}, u32[]{:S(2)}, u32[]{:S(2)}) collective-permute-start(bf16[4,2,128,128]{3,2,1,0:T(8,128)(2,1)S(1)} %shard_map.56.refs_0_), channel_id=1, source_target_pairs={{0,28},{4,0},{8,4},{12,8},{16,12},{20,16},{24,20},{28,24},{1,29},{... | collective-permute-start | bytes 786440 | tf_op jit(solution)/shard_map/ppermute | solution.py:275
  19.8 0.9 %shard_map.58 = bf16[16,128,128]{2,1,0:T(8,128)(2,1)} custom-call(bf16[128,512]{1,0:T(8,128)(2,1)S(1)} %collective-permute-done.q_ref), custom_call_target="tpu_custom_call" | custom-call | flops 1024 | bytes 1024 | tf_op jit(solution)/shard_map/pallas_call | solution.py:266
  20.7 6.2 %all-to-all-start = ((bf16[16,128,128]{2,1,0:T(8,128)(2,1)}), bf16[16,128,128]{2,1,0:T(8,128)(2,1)S(1)}, u32[]{:S(2)}, u32[]{:S(2)}) async-start(bf16[16,128,128]{2,1,0:T(8,128)(2,1)} %shard_map.58), calls=%async_computation | async-start | bytes 1048576 | tf_op jit(solution)/shard_map/all_to_all | solution.py:274
  26.9 0.0 collective-permute-done.4.refs_1_
  26.9 0.1 collective-permute-start.6
  27.0 0.0 copy-done.1
  27.0 0.1 select_reduce_fusion.2
  27.1 0.0 copy-done
  27.1 0.1 slice_reduce_fusion.1
  27.3 0.1 select_reduce_fusion.1
  27.4 0.4 fusion.3.need_ref
  27.8 0.6 collective-permute-start.7
  28.4 1.5 %shard_map.57.plan_ref = s32[242]{0:T(256)S(1)} custom-call(s32[16]{0:T(128)S(1)} %fusion.3.need_ref, s32[16]{0:T(128)S(1)} %get-tuple-element.36.qblk_ref, s32[24]{0:T(128)S(1)} %get-tuple-element.38.kblk_ref), custom_call_target="tpu_custom_call" | custom-call | flops 1024 | bytes 1024 | tf_op jit(solution)/shard_map/pallas_call | solution.py:320
  29.9 0.0 collective-permute-done.5.refs_2_
  29.9 0.1 collective-permute-start.8
  30.0 0.1 iota_add_fusion
  30.1 0.1 select_reduce_fusion.start_ref
  30.2 0.0 collective-permute-done.6.refs_3_
  30.2 0.0 collective-permute-done.7.refs_4_
  30.2 1.3 %collective-permute-done.8.refs_5_ = bf16[4,2,128,128]{3,2,1,0:T(8,128)(2,1)S(1)} collective-permute-done((bf16[4,2,128,128]{3,2,1,0:T(8,128)(2,1)S(1)}, bf16[4,2,128,128]{3,2,1,0:T(8,128)(2,1)S(1)}, u32[]{:S(2)}, u32[]{:S(2)}) %collective-permute-start.8) | collective-permute-done | bytes 262176 | tf_op jit(solution)/shard_map/ppermute | solution.py:279
  31.5 0.1 shard_map.59.kv_ref
  31.7 5.2 %all-to-all-done.q_ref = bf16[16,128,128]{2,1,0:T(8,128)(2,1)S(1)} async-done(((bf16[16,128,128]{2,1,0:T(8,128)(2,1)}), bf16[16,128,128]{2,1,0:T(8,128)(2,1)S(1)}, u32[]{:S(2)}, u32[]{:S(2)}) %all-to-all-start) | async-done | bytes 524320 | tf_op jit(solution)/shard_map/all_to_all | solution.py:274
  36.9 2.8 %shard_map.60 = bf16[16,144,128]{2,1,0:T(8,128)(2,1)S(1)} custom-call(s32[242]{0:T(256)S(1)} %shard_map.57.plan_ref, s32[16,128]{1,0:T(8,128)S(1)} %select_reduce_fusion.start_ref, bf16[16,128,128]{2,1,0:T(8,128)(2,1)S(1)} %all-to-all-done.q_ref, bf16[24,2,128,128]{3,2,1,0:T(8,128)(2,1)S(1)} %shard_map.59.kv_ref), custom_call_target="tpu_custom_call" | custom-call | tf_op jit(solution)/shard_map/pallas_call | solution.py:328
  39.7 13.8 %all_to_all.10.parts_ref = bf16[16,144,128]{2,1,0:T(8,128)(2,1)S(1)} all-to-all(bf16[16,144,128]{2,1,0:T(8,128)(2,1)S(1)} %shard_map.60), channel_id=1, replica_groups=mesh['x'=4,'c'=2,'z'=8,'y'=4] {'x','y'}, dimensions={0} | all-to-all | bytes 1179648 | tf_op jit(solution)/shard_map/all_to_all | solution.py:341
  53.5 0.2 shard_map.61
  53.7 0.1 collective-permute-start.9
  53.8 8.1 %collective-permute-done.9 = bf16[128,512]{1,0:T(8,128)(2,1)S(1)} collective-permute-done((bf16[128,512]{1,0:T(8,128)(2,1)S(1)}, bf16[128,512]{1,0:T(8,128)(2,1)S(1)}, u32[]{:S(2)}, u32[]{:S(2)}) %collective-permute-start.9) | collective-permute-done | bytes 131104 | tf_op jit(solution)/shard_map/ppermute | solution.py:350
  61.9 0.7 %copy.7 = bf16[128,512]{1,0:T(8,128)(2,1)} copy(bf16[128,512]{1,0:T(8,128)(2,1)S(1)} %collective-permute-done.9) | data formatting | bytes 262144
  (4 shorter events, 0.1 us)
Async XLA Ops:
  0.0 27.1 %copy-start = (s32[6400,2]{0,1:T(2,128)S(1)}, s32[6400,2]{0,1:T(2,128)}, u32[]{:S(2)}) copy-start(s32[6400,2]{0,1:T(2,128)} %param.8) | copy-start | bytes 153604
  0.0 27.0 %copy-start.1 = (s32[16]{0:T(128)S(1)}, s32[16]{0:T(128)}, u32[]{:S(2)}) copy-start(s32[16]{0:T(128)} %param.9) | copy-start | bytes 196
  0.0 16.5 %collective-permute-start = (bf16[128,512]{1,0:T(8,128)(2,1)}, bf16[128,512]{1,0:T(8,128)(2,1)S(1)}, u32[]{:S(2)}, u32[]{:S(2)}) collective-permute-start(bf16[128,512]{1,0:T(8,128)(2,1)} %param.5), channel_id=1, source_target_pairs={{0,188},{1,189},{2,190},{3,191},{4,124},{5,125},{6,126},{7,127},{8... | collective-permute-start | bytes 393224 | tf_op jit(solution)/shard_map/ppermute | solution.py:261
  8.9 5.0 %collective-permute-start.1 = (bf16[2,128,128]{2,1,0:T(8,128)(2,1)S(1)}, bf16[2,128,128]{2,1,0:T(8,128)(2,1)S(1)}, u32[]{:S(2)}, u32[]{:S(2)}) collective-permute-start(bf16[2,128,128]{2,1,0:T(8,128)(2,1)S(1)} %get-tuple-element.20), channel_id=1, source_target_pairs={{0,1},{1,2},{2,3},{3,0},{4,5},{5,6},{6,7},{7,4},{8,9},{9,10},{10,1... | collective-permute-start | bytes 196616 | tf_op jit(solution)/shard_map/ppermute | solution.py:262
  10.5 5.9 %collective-permute-start.2 = (bf16[2,128,128]{2,1,0:T(8,128)(2,1)S(1)}, bf16[2,128,128]{2,1,0:T(8,128)(2,1)S(1)}, u32[]{:S(2)}, u32[]{:S(2)}) collective-permute-start(bf16[2,128,128]{2,1,0:T(8,128)(2,1)S(1)} %get-tuple-element.21), channel_id=1, source_target_pairs={{0,2},{1,3},{2,0},{3,1},{4,6},{5,7},{6,4},{7,5},{8,10},{9,11},{10,... | collective-permute-start | bytes 196616 | tf_op jit(solution)/shard_map/ppermute | solution.py:262
  11.5 5.0 %collective-permute-start.3 = (bf16[2,128,128]{2,1,0:T(8,128)(2,1)S(1)}, bf16[2,128,128]{2,1,0:T(8,128)(2,1)S(1)}, u32[]{:S(2)}, u32[]{:S(2)}) collective-permute-start(bf16[2,128,128]{2,1,0:T(8,128)(2,1)S(1)} %get-tuple-element.22), channel_id=1, source_target_pairs={{0,3},{1,0},{2,1},{3,2},{4,7},{5,4},{6,5},{7,6},{8,11},{9,8},{10,9... | collective-permute-start | bytes 196616 | tf_op jit(solution)/shard_map/ppermute | solution.py:262
  16.5 10.4 %collective-permute-start.4 = (bf16[4,2,128,128]{3,2,1,0:T(8,128)(2,1)S(1)}, bf16[4,2,128,128]{3,2,1,0:T(8,128)(2,1)S(1)}, u32[]{:S(2)}, u32[]{:S(2)}) collective-permute-start(bf16[4,2,128,128]{3,2,1,0:T(8,128)(2,1)S(1)} %shard_map.56.refs_0_), channel_id=1, source_target_pairs={{0,4},{4,8},{8,12},{12,16},{16,20},{20,24},{24,28},{28,0},{1,5},{5... | collective-permute-start | bytes 786440 | tf_op jit(solution)/shard_map/ppermute | solution.py:275
  16.6 13.3 %collective-permute-start.5 = (bf16[4,2,128,128]{3,2,1,0:T(8,128)(2,1)S(1)}, bf16[4,2,128,128]{3,2,1,0:T(8,128)(2,1)S(1)}, u32[]{:S(2)}, u32[]{:S(2)}) collective-permute-start(bf16[4,2,128,128]{3,2,1,0:T(8,128)(2,1)S(1)} %shard_map.56.refs_0_), channel_id=1, source_target_pairs={{0,28},{4,0},{8,4},{12,8},{16,12},{20,16},{24,20},{28,24},{1,29},{... | collective-permute-start | bytes 786440 | tf_op jit(solution)/shard_map/ppermute | solution.py:275
  20.7 16.2 %all-to-all-start = ((bf16[16,128,128]{2,1,0:T(8,128)(2,1)}), bf16[16,128,128]{2,1,0:T(8,128)(2,1)S(1)}, u32[]{:S(2)}, u32[]{:S(2)}) async-start(bf16[16,128,128]{2,1,0:T(8,128)(2,1)} %shard_map.58), calls=%async_computation | async-start | bytes 1048576 | tf_op jit(solution)/shard_map/all_to_all | solution.py:274
  26.9 3.3 %collective-permute-start.6 = (bf16[4,2,128,128]{3,2,1,0:T(8,128)(2,1)S(1)}, bf16[4,2,128,128]{3,2,1,0:T(8,128)(2,1)S(1)}, u32[]{:S(2)}, u32[]{:S(2)}) collective-permute-start(bf16[4,2,128,128]{3,2,1,0:T(8,128)(2,1)S(1)} %shard_map.56.refs_0_), channel_id=1, source_target_pairs={{0,32},{32,0},{1,33},{33,1},{2,34},{34,2},{3,35},{35,3},{4,36},{36... | collective-permute-start | bytes 786440 | tf_op jit(solution)/shard_map/ppermute | solution.py:279
  27.8 2.4 %collective-permute-start.7 = (bf16[4,2,128,128]{3,2,1,0:T(8,128)(2,1)S(1)}, bf16[4,2,128,128]{3,2,1,0:T(8,128)(2,1)S(1)}, u32[]{:S(2)}, u32[]{:S(2)}) collective-permute-start(bf16[4,2,128,128]{3,2,1,0:T(8,128)(2,1)S(1)} %collective-permute-done.4.refs_1_), channel_id=1, source_target_pairs={{0,32},{32,0},{1,33},{33,1},{2,34},{34,2},{3,35},{35,3},{4,36},{36... | collective-permute-start | bytes 786440 | tf_op jit(solution)/shard_map/ppermute | solution.py:279
  29.9 1.6 %collective-permute-start.8 = (bf16[4,2,128,128]{3,2,1,0:T(8,128)(2,1)S(1)}, bf16[4,2,128,128]{3,2,1,0:T(8,128)(2,1)S(1)}, u32[]{:S(2)}, u32[]{:S(2)}) collective-permute-start(bf16[4,2,128,128]{3,2,1,0:T(8,128)(2,1)S(1)} %collective-permute-done.5.refs_2_), channel_id=1, source_target_pairs={{0,32},{32,0},{1,33},{33,1},{2,34},{34,2},{3,35},{35,3},{4,36},{36... | collective-permute-start | bytes 786440 | tf_op jit(solution)/shard_map/ppermute | solution.py:279
  53.7 8.2 %collective-permute-start.9 = (bf16[128,512]{1,0:T(8,128)(2,1)S(1)}, bf16[128,512]{1,0:T(8,128)(2,1)S(1)}, u32[]{:S(2)}, u32[]{:S(2)}) collective-permute-start(bf16[128,512]{1,0:T(8,128)(2,1)S(1)} %shard_map.61), channel_id=1, source_target_pairs={{188,0},{189,1},{190,2},{191,3},{124,4},{125,5},{126,6},{127,7},{6... | collective-permute-start | bytes 393224 | tf_op jit(solution)/shard_map/ppermute | solution.py:350

commit v2 on v0

--- a/solution.py
+++ b/solution.py
@@ -71,7 +71,7 @@
 
 def pack_queries_kernel(q_ref, out_ref):
     for h in range(H):
-        part = q_ref[:, h * DH : (h + 1) * DH].astype(jnp.float32).T.astype(jnp.bfloat16)
+        part = q_ref[:, h * DH : (h + 1) * DH].T
         for x in range(NX):
             out_ref[x * H + h] = part
 

time: 62.9 us -> 62.1 us (0.987)
  transfers between devices with their start and end apart: 11 -> 11, of which waited for: 4 -> 4; matrix products, arithmetic and copies ran while one was open for 1% -> 2% of each run, Pallas kernels for 6% -> 6%
where the time goes in v2:
time: 62.1 us; the launch traced here: 61.9 us
  starting transfers between devices  23.1 us (37%)
  waiting for transfers between devices  17.4 us (28%)
  blocking collectives  14.4 us (23%)
  Pallas kernels  5.26 us (8%)
  local copies, waits for them, and re-layouts  0.78 us (1%)
    all_to_all x1, blocking collectives, on_device(): gathered = lax.all_to_all(parts, ('x', 'y'), 0, 0, tiled=True)  14.4 us
    ppermute x1, waiting for transfers between devices, on_device(): return lax.ppermute(result, ('x', 'c', 'z', 'y'), transpose_pairs(True))  8.22 us
    ppermute x1, starting transfers between devices, on_device(): moved = lax.ppermute(queries, ('x', 'c', 'z', 'y'), transpose_pairs(False))  7.76 us
    all_to_all x1, starting transfers between devices, on_device(): mine = lax.all_to_all(spread, ('x', 'y'), 0, 0, tiled=True)  6.18 us
    all_to_all x1, waiting for transfers between devices, on_device(): mine = lax.all_to_all(spread, ('x', 'y'), 0, 0, tiled=True)  5.33 us
    ppermute x3, starting transfers between devices, on_device(): lax.ppermute(split[d], 'y', ring(NY, d))  5 us
    ppermute x1, starting transfers between devices, on_device(): lax.ppermute(here, 'z', ring(NZ, -1))  3.21 us
    ppermute x3, waiting for transfers between devices, on_device(): lax.ppermute(split[d], 'y', ring(NY, d))  2.56 us
  transfers between devices with their start and end apart: 11, of which 4 were waited for; matrix products, arithmetic and copies ran while one was open for 2% of the time, Pallas kernels for 6%

profile of v2, /device:TPU:8, one launch (start us, length us, event | category | flops | bytes accessed | tf_op | source)
XLA Modules:
  0.0 61.9 jit_solution(17860630035323796487)
XLA Ops:
  0.0 0.0 copy-start
  0.0 0.0 copy-start.1
  0.0 7.8 %collective-permute-start = (bf16[128,512]{1,0:T(8,128)(2,1)}, bf16[128,512]{1,0:T(8,128)(2,1)S(1)}, u32[]{:S(2)}, u32[]{:S(2)}) collective-permute-start(bf16[128,512]{1,0:T(8,128)(2,1)} %param.5), channel_id=1, source_target_pairs={{0,188},{1,189},{2,190},{3,191},{4,124},{5,125},{6,126},{7,127},{8... | collective-permute-start | bytes 393224 | tf_op jit(solution)/shard_map/ppermute | solution.py:261
  7.8 1.1 %shard_map.55 = (bf16[2,128,128]{2,1,0:T(8,128)(2,1)S(1)}, bf16[2,128,128]{2,1,0:T(8,128)(2,1)S(1)}, bf16[2,128,128]{2,1,0:T(8,128)(2,1)S(1)}, bf16[2,128,128]{2,1,0:T(8,128)(2,1)S(1)}) custom-call(s32[1]{0:T(128)} %bitcast.y_ref, bf16[128,512]{1,0:T(8,128)(2,1)} %k_hbm.1, bf16[128,512]{1,0:T(8,128)(2,1)} %v_hbm.1), custom_call_target="tpu_custom_call" | custom-call | flops 1024 | bytes 1024 | tf_op jit(solution)/shard_map/pallas_call | solution.py:248
  8.9 1.7 %collective-permute-start.1 = (bf16[2,128,128]{2,1,0:T(8,128)(2,1)S(1)}, bf16[2,128,128]{2,1,0:T(8,128)(2,1)S(1)}, u32[]{:S(2)}, u32[]{:S(2)}) collective-permute-start(bf16[2,128,128]{2,1,0:T(8,128)(2,1)S(1)} %get-tuple-element.20), channel_id=1, source_target_pairs={{0,1},{1,2},{2,3},{3,0},{4,5},{5,6},{6,7},{7,4},{8,9},{9,10},{10,1... | collective-permute-start | bytes 196616 | tf_op jit(solution)/shard_map/ppermute | solution.py:262
  10.5 0.9 %collective-permute-start.2 = (bf16[2,128,128]{2,1,0:T(8,128)(2,1)S(1)}, bf16[2,128,128]{2,1,0:T(8,128)(2,1)S(1)}, u32[]{:S(2)}, u32[]{:S(2)}) collective-permute-start(bf16[2,128,128]{2,1,0:T(8,128)(2,1)S(1)} %get-tuple-element.21), channel_id=1, source_target_pairs={{0,2},{1,3},{2,0},{3,1},{4,6},{5,7},{6,4},{7,5},{8,10},{9,11},{10,... | collective-permute-start | bytes 196616 | tf_op jit(solution)/shard_map/ppermute | solution.py:262
  11.5 2.4 %collective-permute-start.3 = (bf16[2,128,128]{2,1,0:T(8,128)(2,1)S(1)}, bf16[2,128,128]{2,1,0:T(8,128)(2,1)S(1)}, u32[]{:S(2)}, u32[]{:S(2)}) collective-permute-start(bf16[2,128,128]{2,1,0:T(8,128)(2,1)S(1)} %get-tuple-element.22), channel_id=1, source_target_pairs={{0,3},{1,0},{2,1},{3,2},{4,7},{5,4},{6,5},{7,6},{8,11},{9,8},{10,9... | collective-permute-start | bytes 196616 | tf_op jit(solution)/shard_map/ppermute | solution.py:262
  13.9 0.0 collective-permute-done.1
  13.9 2.5 %collective-permute-done.2 = bf16[2,128,128]{2,1,0:T(8,128)(2,1)S(1)} collective-permute-done((bf16[2,128,128]{2,1,0:T(8,128)(2,1)S(1)}, bf16[2,128,128]{2,1,0:T(8,128)(2,1)S(1)}, u32[]{:S(2)}, u32[]{:S(2)}) %collective-permute-start.2) | collective-permute-done | bytes 65568 | tf_op jit(solution)/shard_map/ppermute | solution.py:262
  16.4 0.0 collective-permute-done.3
  16.5 0.0 collective-permute-done.q_ref
  16.5 0.1 collective-permute-start.4
  16.6 3.2 %collective-permute-start.5 = (bf16[4,2,128,128]{3,2,1,0:T(8,128)(2,1)S(1)}, bf16[4,2,128,128]{3,2,1,0:T(8,128)(2,1)S(1)}, u32[]{:S(2)}, u32[]{:S(2)}) collective-permute-start(bf16[4,2,128,128]{3,2,1,0:T(8,128)(2,1)S(1)} %shard_map.56.refs_0_), channel_id=1, source_target_pairs={{0,28},{4,0},{8,4},{12,8},{16,12},{20,16},{24,20},{28,24},{1,29},{... | collective-permute-start | bytes 786440 | tf_op jit(solution)/shard_map/ppermute | solution.py:275
  19.8 0.9 %shard_map.58 = bf16[16,128,128]{2,1,0:T(8,128)(2,1)} custom-call(bf16[128,512]{1,0:T(8,128)(2,1)S(1)} %collective-permute-done.q_ref), custom_call_target="tpu_custom_call" | custom-call | flops 1024 | bytes 1024 | tf_op jit(solution)/shard_map/pallas_call | solution.py:266
  20.7 6.2 %all-to-all-start = ((bf16[16,128,128]{2,1,0:T(8,128)(2,1)}), bf16[16,128,128]{2,1,0:T(8,128)(2,1)S(1)}, u32[]{:S(2)}, u32[]{:S(2)}) async-start(bf16[16,128,128]{2,1,0:T(8,128)(2,1)} %shard_map.58), calls=%async_computation | async-start | bytes 1048576 | tf_op jit(solution)/shard_map/all_to_all | solution.py:274
  26.9 0.0 collective-permute-done.4.refs_1_
  26.9 0.1 collective-permute-start.6
  27.0 0.0 copy-done.1
  27.0 0.1 select_reduce_fusion.2
  27.1 0.0 copy-done
  27.1 0.1 slice_reduce_fusion.1
  27.3 0.1 select_reduce_fusion.1
  27.4 0.4 fusion.3.need_ref
  27.8 0.6 collective-permute-start.7
  28.4 1.4 %shard_map.57.plan_ref = s32[242]{0:T(256)S(1)} custom-call(s32[16]{0:T(128)S(1)} %fusion.3.need_ref, s32[16]{0:T(128)S(1)} %get-tuple-element.36.qblk_ref, s32[24]{0:T(128)S(1)} %get-tuple-element.38.kblk_ref), custom_call_target="tpu_custom_call" | custom-call | flops 1024 | bytes 1024 | tf_op jit(solution)/shard_map/pallas_call | solution.py:320
  29.8 0.0 collective-permute-done.5.refs_2_
  29.8 0.2 collective-permute-start.8
  30.0 0.1 iota_add_fusion
  30.1 0.1 select_reduce_fusion.start_ref
  30.2 0.0 collective-permute-done.6.refs_3_
  30.2 0.0 collective-permute-done.7.refs_4_
  30.2 1.3 %collective-permute-done.8.refs_5_ = bf16[4,2,128,128]{3,2,1,0:T(8,128)(2,1)S(1)} collective-permute-done((bf16[4,2,128,128]{3,2,1,0:T(8,128)(2,1)S(1)}, bf16[4,2,128,128]{3,2,1,0:T(8,128)(2,1)S(1)}, u32[]{:S(2)}, u32[]{:S(2)}) %collective-permute-start.8) | collective-permute-done | bytes 262176 | tf_op jit(solution)/shard_map/ppermute | solution.py:279
  31.5 0.1 shard_map.59.kv_ref
  31.6 5.3 %all-to-all-done.q_ref = bf16[16,128,128]{2,1,0:T(8,128)(2,1)S(1)} async-done(((bf16[16,128,128]{2,1,0:T(8,128)(2,1)}), bf16[16,128,128]{2,1,0:T(8,128)(2,1)S(1)}, u32[]{:S(2)}, u32[]{:S(2)}) %all-to-all-start) | async-done | bytes 524320 | tf_op jit(solution)/shard_map/all_to_all | solution.py:274
  36.9 1.5 %shard_map.60 = bf16[16,144,128]{2,1,0:T(8,128)(2,1)S(1)} custom-call(s32[242]{0:T(256)S(1)} %shard_map.57.plan_ref, s32[16,128]{1,0:T(8,128)S(1)} %select_reduce_fusion.start_ref, bf16[16,128,128]{2,1,0:T(8,128)(2,1)S(1)} %all-to-all-done.q_ref, bf16[24,2,128,128]{3,2,1,0:T(8,128)(2,1)S(1)} %shard_map.59.kv_ref), custom_call_target="tpu_custom_call" | custom-call | tf_op jit(solution)/shard_map/pallas_call | solution.py:328
  38.4 14.4 %all_to_all.10.parts_ref = bf16[16,144,128]{2,1,0:T(8,128)(2,1)S(1)} all-to-all(bf16[16,144,128]{2,1,0:T(8,128)(2,1)S(1)} %shard_map.60), channel_id=1, replica_groups=mesh['x'=4,'c'=2,'z'=8,'y'=4] {'x','y'}, dimensions={0} | all-to-all | bytes 1179648 | tf_op jit(solution)/shard_map/all_to_all | solution.py:341
  52.7 0.2 shard_map.61
  52.9 0.1 collective-permute-start.9
  53.0 8.2 %collective-permute-done.9 = bf16[128,512]{1,0:T(8,128)(2,1)S(1)} collective-permute-done((bf16[128,512]{1,0:T(8,128)(2,1)S(1)}, bf16[128,512]{1,0:T(8,128)(2,1)S(1)}, u32[]{:S(2)}, u32[]{:S(2)}) %collective-permute-start.9) | collective-permute-done | bytes 131104 | tf_op jit(solution)/shard_map/ppermute | solution.py:350
  61.3 0.7 %copy.7 = bf16[128,512]{1,0:T(8,128)(2,1)} copy(bf16[128,512]{1,0:T(8,128)(2,1)S(1)} %collective-permute-done.9) | data formatting | bytes 262144
  (4 shorter events, 0.1 us)
Async XLA Ops:
  0.0 27.1 %copy-start = (s32[6400,2]{0,1:T(2,128)S(1)}, s32[6400,2]{0,1:T(2,128)}, u32[]{:S(2)}) copy-start(s32[6400,2]{0,1:T(2,128)} %param.8) | copy-start | bytes 153604
  0.0 27.0 %copy-start.1 = (s32[16]{0:T(128)S(1)}, s32[16]{0:T(128)}, u32[]{:S(2)}) copy-start(s32[16]{0:T(128)} %param.9) | copy-start | bytes 196
  0.0 16.5 %collective-permute-start = (bf16[128,512]{1,0:T(8,128)(2,1)}, bf16[128,512]{1,0:T(8,128)(2,1)S(1)}, u32[]{:S(2)}, u32[]{:S(2)}) collective-permute-start(bf16[128,512]{1,0:T(8,128)(2,1)} %param.5), channel_id=1, source_target_pairs={{0,188},{1,189},{2,190},{3,191},{4,124},{5,125},{6,126},{7,127},{8... | collective-permute-start | bytes 393224 | tf_op jit(solution)/shard_map/ppermute | solution.py:261
  8.9 5.0 %collective-permute-start.1 = (bf16[2,128,128]{2,1,0:T(8,128)(2,1)S(1)}, bf16[2,128,128]{2,1,0:T(8,128)(2,1)S(1)}, u32[]{:S(2)}, u32[]{:S(2)}) collective-permute-start(bf16[2,128,128]{2,1,0:T(8,128)(2,1)S(1)} %get-tuple-element.20), channel_id=1, source_target_pairs={{0,1},{1,2},{2,3},{3,0},{4,5},{5,6},{6,7},{7,4},{8,9},{9,10},{10,1... | collective-permute-start | bytes 196616 | tf_op jit(solution)/shard_map/ppermute | solution.py:262
  10.5 5.9 %collective-permute-start.2 = (bf16[2,128,128]{2,1,0:T(8,128)(2,1)S(1)}, bf16[2,128,128]{2,1,0:T(8,128)(2,1)S(1)}, u32[]{:S(2)}, u32[]{:S(2)}) collective-permute-start(bf16[2,128,128]{2,1,0:T(8,128)(2,1)S(1)} %get-tuple-element.21), channel_id=1, source_target_pairs={{0,2},{1,3},{2,0},{3,1},{4,6},{5,7},{6,4},{7,5},{8,10},{9,11},{10,... | collective-permute-start | bytes 196616 | tf_op jit(solution)/shard_map/ppermute | solution.py:262
  11.5 5.0 %collective-permute-start.3 = (bf16[2,128,128]{2,1,0:T(8,128)(2,1)S(1)}, bf16[2,128,128]{2,1,0:T(8,128)(2,1)S(1)}, u32[]{:S(2)}, u32[]{:S(2)}) collective-permute-start(bf16[2,128,128]{2,1,0:T(8,128)(2,1)S(1)} %get-tuple-element.22), channel_id=1, source_target_pairs={{0,3},{1,0},{2,1},{3,2},{4,7},{5,4},{6,5},{7,6},{8,11},{9,8},{10,9... | collective-permute-start | bytes 196616 | tf_op jit(solution)/shard_map/ppermute | solution.py:262
  16.5 10.4 %collective-permute-start.4 = (bf16[4,2,128,128]{3,2,1,0:T(8,128)(2,1)S(1)}, bf16[4,2,128,128]{3,2,1,0:T(8,128)(2,1)S(1)}, u32[]{:S(2)}, u32[]{:S(2)}) collective-permute-start(bf16[4,2,128,128]{3,2,1,0:T(8,128)(2,1)S(1)} %shard_map.56.refs_0_), channel_id=1, source_target_pairs={{0,4},{4,8},{8,12},{12,16},{16,20},{20,24},{24,28},{28,0},{1,5},{5... | collective-permute-start | bytes 786440 | tf_op jit(solution)/shard_map/ppermute | solution.py:275
  16.6 13.2 %collective-permute-start.5 = (bf16[4,2,128,128]{3,2,1,0:T(8,128)(2,1)S(1)}, bf16[4,2,128,128]{3,2,1,0:T(8,128)(2,1)S(1)}, u32[]{:S(2)}, u32[]{:S(2)}) collective-permute-start(bf16[4,2,128,128]{3,2,1,0:T(8,128)(2,1)S(1)} %shard_map.56.refs_0_), channel_id=1, source_target_pairs={{0,28},{4,0},{8,4},{12,8},{16,12},{20,16},{24,20},{28,24},{1,29},{... | collective-permute-start | bytes 786440 | tf_op jit(solution)/shard_map/ppermute | solution.py:275
  20.7 16.2 %all-to-all-start = ((bf16[16,128,128]{2,1,0:T(8,128)(2,1)}), bf16[16,128,128]{2,1,0:T(8,128)(2,1)S(1)}, u32[]{:S(2)}, u32[]{:S(2)}) async-start(bf16[16,128,128]{2,1,0:T(8,128)(2,1)} %shard_map.58), calls=%async_computation | async-start | bytes 1048576 | tf_op jit(solution)/shard_map/all_to_all | solution.py:274
  26.9 3.3 %collective-permute-start.6 = (bf16[4,2,128,128]{3,2,1,0:T(8,128)(2,1)S(1)}, bf16[4,2,128,128]{3,2,1,0:T(8,128)(2,1)S(1)}, u32[]{:S(2)}, u32[]{:S(2)}) collective-permute-start(bf16[4,2,128,128]{3,2,1,0:T(8,128)(2,1)S(1)} %shard_map.56.refs_0_), channel_id=1, source_target_pairs={{0,32},{32,0},{1,33},{33,1},{2,34},{34,2},{3,35},{35,3},{4,36},{36... | collective-permute-start | bytes 786440 | tf_op jit(solution)/shard_map/ppermute | solution.py:279
  27.8 2.4 %collective-permute-start.7 = (bf16[4,2,128,128]{3,2,1,0:T(8,128)(2,1)S(1)}, bf16[4,2,128,128]{3,2,1,0:T(8,128)(2,1)S(1)}, u32[]{:S(2)}, u32[]{:S(2)}) collective-permute-start(bf16[4,2,128,128]{3,2,1,0:T(8,128)(2,1)S(1)} %collective-permute-done.4.refs_1_), channel_id=1, source_target_pairs={{0,32},{32,0},{1,33},{33,1},{2,34},{34,2},{3,35},{35,3},{4,36},{36... | collective-permute-start | bytes 786440 | tf_op jit(solution)/shard_map/ppermute | solution.py:279
  29.8 1.6 %collective-permute-start.8 = (bf16[4,2,128,128]{3,2,1,0:T(8,128)(2,1)S(1)}, bf16[4,2,128,128]{3,2,1,0:T(8,128)(2,1)S(1)}, u32[]{:S(2)}, u32[]{:S(2)}) collective-permute-start(bf16[4,2,128,128]{3,2,1,0:T(8,128)(2,1)S(1)} %collective-permute-done.5.refs_2_), channel_id=1, source_target_pairs={{0,32},{32,0},{1,33},{33,1},{2,34},{34,2},{3,35},{35,3},{4,36},{36... | collective-permute-start | bytes 786440 | tf_op jit(solution)/shard_map/ppermute | solution.py:279
  52.9 8.3 %collective-permute-start.9 = (bf16[128,512]{1,0:T(8,128)(2,1)S(1)}, bf16[128,512]{1,0:T(8,128)(2,1)S(1)}, u32[]{:S(2)}, u32[]{:S(2)}) collective-permute-start(bf16[128,512]{1,0:T(8,128)(2,1)S(1)} %shard_map.61), channel_id=1, source_target_pairs={{188,0},{189,1},{190,2},{191,3},{124,4},{125,5},{126,6},{127,7},{6... | collective-permute-start | bytes 393224 | tf_op jit(solution)/shard_map/ppermute | solution.py:350
